TPU v7x, 32 devices: a whole 2x2x4 slice. The times are simulated.
32 devices in a mesh: dp: 4 (over x, core), head: 4 (over z), expert: 2 (over y).
Axes of the slice: x: 2, y: 2, z: 4, core: 2. Of those that a mesh axis runs over, the one named last changes fastest.
Arguments:
- tokens: bfloat16 [4, 64, 4096], P('dp', ('head', 'expert')), may hold values from -6 to 6
- cotangent: bfloat16 [4, 64, 4096], P('dp', ('head', 'expert')), may hold values from -1.5 to 1.5
- queries: bfloat16 [4, 64, 32, 128], P('dp', 'expert', 'head'), may hold values from -32 to 32
- key_vectors: bfloat16 [4, 64, 32, 128], P('dp', 'expert', 'head'), may hold values from -32 to 32
- value_routes: int32 [4, 32, 64, 1], P('dp', 'head'), may hold values from 0 to 3; in each aligned block of 8 rows (0 to 7, 8 to 15, ..., all dimensions but the last counted through in order) at most 3 rows name the same one
- output_routes: int32 [4, 32, 64, 1], P('dp', 'head'), may hold values from 0 to 3; in each aligned block of 8 rows (0 to 7, 8 to 15, ..., all dimensions but the last counted through in order) at most 3 rows name the same one
- value_experts: bfloat16 [128, 4096, 128], P(('head', 'expert')), may hold values from -0.09375 to 0.09375
- output_experts: bfloat16 [128, 4096, 128], P(('head', 'expert')), may hold values from -0.09375 to 0.09375
Outputs:
- token_grads: bfloat16 [4, 64, 4096], P('dp', ('head', 'expert'))
- query_grads: bfloat16 [4, 64, 32, 128], P('dp', 'expert', 'head')
- key_grads: bfloat16 [4, 64, 32, 128], P('dp', 'expert', 'head')
- value_grads: bfloat16 [128, 4096, 128], P(('head', 'expert'), 'dp')
- output_grads: bfloat16 [128, 4096, 128], P(('head', 'expert'), 'dp')
Inputs may be any that keep to these rules, and one draw needn't show every extreme that they name: value_routes[b, h, t, 0] is the value expert of head h for token t. In each aligned block of 8 tokens of one sequence and head, no expert is chosen more than 3 times, and in every draw some block has exactly 3 for one expert. output_routes[b, h, t, 0] is the output expert of head h for token t. In each aligned block of 8 tokens of one sequence and head, no expert is chosen more than 3 times, and in every draw some block has exactly 3 for one expert.
All inputs are finite; a program needn't handle non-finite values.
Results may differ from a plain program's by a relative error of at most 0.028.
Values may be sent and summed in bfloat16 or wider, within the bound.
A program may use at most 128 MiB of HBM per device.

v0:
```python
import jax
import jax.numpy as jnp
from jax import lax
from jax.sharding import PartitionSpec as P

E = 4
CAP = 3


def slot_rank(routes):
    onehot = (routes[..., None] == jnp.arange(E, dtype=jnp.int32)).astype(jnp.int32)
    before = jnp.cumsum(onehot, axis=-2) - onehot
    return jnp.sum(before * onehot, axis=-1)


def slot_table(routes):
    rank_of = slot_rank(routes)
    expert_hit = routes[..., None, None, :] == jnp.arange(E, dtype=jnp.int32)[:, None, None]
    place_hit = rank_of[..., None, None, :] == jnp.arange(CAP, dtype=jnp.int32)[:, None]
    return jnp.logical_and(expert_hit, place_hit).astype(jnp.bfloat16)


def local(
    tokens,
    cotangent,
    queries,
    key_vectors,
    value_routes,
    output_routes,
    value_experts,
    output_experts,
):
    head_count = lax.axis_size("head")
    expert_count = lax.axis_size("expert")
    sources = head_count * expert_count
    expert_index = lax.axis_index("expert")
    tok_rows = tokens.shape[1]
    model_width = tokens.shape[2]
    query_rows = queries.shape[1]
    groups = queries.shape[2]
    head_dim = queries.shape[3]
    seq_len = value_routes.shape[2]
    pairs_dev = value_experts.shape[0]
    slot_count = sources * CAP
    score_scale = head_dim ** (-0.5)
    value_local = value_routes[0, :, :, 0]
    output_local = output_routes[0, :, :, 0]

    def own_block(route_part):
        shaped = route_part.reshape(groups, head_count, expert_count, tok_rows)
        return lax.dynamic_index_in_dim(shaped, expert_index, 2, keepdims=False)

    own_pair = jnp.stack([own_block(value_local), own_block(output_local)])
    own_routes = lax.all_to_all(own_pair, "head", split_axis=2, concat_axis=1, tiled=True).reshape(
        2, groups * head_count, tok_rows
    )
    value_table = slot_table(own_routes[0]).reshape(
        head_count, expert_count, pairs_dev, CAP, tok_rows
    )

    def pair_rows(route_part, gathered):
        slot_map = slot_table(route_part.reshape(groups, sources, tok_rows))
        slot_map = jnp.moveaxis(slot_map, 2, 1).reshape(groups * E, sources, CAP, tok_rows)
        slot_map = lax.dynamic_slice_in_dim(slot_map, expert_index * pairs_dev, pairs_dev, 0)
        picked = jnp.einsum(
            "psmt,stw->psmw",
            slot_map,
            gathered.reshape(sources, tok_rows, model_width),
            preferred_element_type=jnp.float32,
        )
        return picked.astype(jnp.bfloat16).reshape(pairs_dev, slot_count, model_width)

    whole_tokens, whole_cotangent = (
        lax.all_gather(tokens[0], ("head", "expert"), axis=0, tiled=True),
        lax.all_gather(cotangent[0], ("head", "expert"), axis=0, tiled=True),
    )
    token_slots = pair_rows(value_local, whole_tokens)
    cotangent_slots = pair_rows(output_local, whole_cotangent)
    value_slots = jnp.einsum(
        "prw,pwk->prk", token_slots, value_experts, preferred_element_type=jnp.float32
    ).astype(jnp.bfloat16)
    upstream_slots = jnp.einsum(
        "prw,pwk->prk", cotangent_slots, output_experts, preferred_element_type=jnp.float32
    ).astype(jnp.bfloat16)
    query_start = expert_index * query_rows
    group_values, group_upstream, all_keys = (
        lax.all_gather(value_slots, "expert", axis=0, tiled=True),
        lax.all_gather(upstream_slots, "expert", axis=0, tiled=True),
        lax.all_gather(key_vectors[0], "expert", axis=0, tiled=True),
    )
    token_source = jnp.arange(seq_len, dtype=jnp.int32) // tok_rows
    head_base = jnp.arange(groups, dtype=jnp.int32)[:, None] * E
    value_rank = slot_rank(value_local.reshape(groups, sources, tok_rows)).reshape(groups, seq_len)
    value_index = (head_base + value_local) * slot_count + token_source * CAP + value_rank
    value_rows = group_values.reshape(-1, head_dim)[value_index]
    output_rank = slot_rank(output_local.reshape(groups, sources, tok_rows)).reshape(
        groups, seq_len
    )
    block_routes = lax.dynamic_slice_in_dim(output_local, query_start, query_rows, 1)
    block_rank = lax.dynamic_slice_in_dim(output_rank, query_start, query_rows, 1)
    block_source = lax.dynamic_slice_in_dim(token_source, query_start, query_rows, 0)
    upstream_index = (head_base + block_routes) * slot_count + block_source * CAP + block_rank
    upstream_rows = group_upstream.reshape(-1, head_dim)[upstream_index]
    query_own = queries[0]
    scores = (
        jnp.einsum("ihc,jhc->hij", query_own, all_keys, preferred_element_type=jnp.float32)
        * score_scale
    )
    query_pos = query_start + jnp.arange(query_rows, dtype=jnp.int32)
    causal = jnp.arange(seq_len, dtype=jnp.int32)[None, :] <= query_pos[:, None]
    row_top = jnp.max(jnp.where(causal, scores, -jnp.inf), axis=-1, keepdims=True)
    weights = jnp.where(causal, jnp.exp(scores - row_top), 0.0)
    probs_full = weights / jnp.sum(weights, axis=-1, keepdims=True)
    prob_half = probs_full.astype(jnp.bfloat16)
    outputs = jnp.einsum(
        "hij,hjc->hic", prob_half, value_rows, preferred_element_type=jnp.float32
    ).astype(jnp.bfloat16)
    row_delta = jnp.sum(outputs.astype(jnp.float32) * upstream_rows.astype(jnp.float32), axis=-1)
    prob_grads = jnp.einsum(
        "hic,hjc->hij", upstream_rows, value_rows, preferred_element_type=jnp.float32
    )
    score_grads = (probs_full * (prob_grads - row_delta[:, :, None])).astype(jnp.bfloat16)
    query_grads = (
        jnp.einsum("hij,jhc->ihc", score_grads, all_keys, preferred_element_type=jnp.float32)
        * score_scale
    ).astype(jnp.bfloat16)
    key_part = (
        jnp.einsum("hij,ihc->jhc", score_grads, query_own, preferred_element_type=jnp.float32)
        * score_scale
    )
    value_part = jnp.einsum(
        "hij,hic->jhc", prob_half, upstream_rows, preferred_element_type=jnp.float32
    )
    key_sum, value_sum = (
        lax.psum_scatter(key_part, "expert", scatter_dimension=0, tiled=True),
        lax.psum_scatter(value_part, "expert", scatter_dimension=0, tiled=True),
    )
    value_half = value_sum.astype(jnp.bfloat16)
    block_value_routes = lax.dynamic_slice_in_dim(value_local, query_start, query_rows, 1).reshape(
        groups, head_count, tok_rows
    )
    value_place = slot_table(block_value_routes)
    output_place = slot_table(block_routes.reshape(groups, head_count, tok_rows))
    value_send = jnp.einsum(
        "hsemt,sthc->hesmc",
        value_place,
        value_half.reshape(head_count, tok_rows, groups, head_dim),
        preferred_element_type=jnp.float32,
    )
    value_send = value_send.astype(jnp.bfloat16).reshape(groups * E, head_count * CAP, head_dim)
    output_send = jnp.einsum(
        "hsemt,hstc->hesmc",
        output_place,
        outputs.reshape(groups, head_count, tok_rows, head_dim),
        preferred_element_type=jnp.float32,
    )
    output_send = output_send.astype(jnp.bfloat16).reshape(groups * E, head_count * CAP, head_dim)
    output_slots, grad_slots = (
        lax.all_to_all(output_send, "expert", split_axis=0, concat_axis=1, tiled=True),
        lax.all_to_all(value_send, "expert", split_axis=0, concat_axis=1, tiled=True),
    )
    value_term = jnp.einsum(
        "prw,prk->pwk", token_slots, grad_slots, preferred_element_type=jnp.float32
    )
    output_term = jnp.einsum(
        "prw,prk->pwk", cotangent_slots, output_slots, preferred_element_type=jnp.float32
    )
    value_grads, output_grads = (
        lax.psum_scatter(
            value_term.astype(jnp.bfloat16), "dp", scatter_dimension=1, tiled=True
        ).astype(jnp.float32),
        lax.psum_scatter(
            output_term.astype(jnp.bfloat16), "dp", scatter_dimension=1, tiled=True
        ).astype(jnp.float32),
    )
    token_terms = jnp.einsum(
        "prk,pwk->prw", grad_slots, value_experts, preferred_element_type=jnp.float32
    ).astype(jnp.bfloat16)
    returned = lax.all_to_all(
        token_terms.reshape(pairs_dev, sources, CAP, model_width),
        ("head", "expert"),
        split_axis=1,
        concat_axis=0,
        tiled=True,
    )
    returned = returned.reshape(head_count, expert_count, pairs_dev, CAP, model_width)
    token_grads = jnp.einsum(
        "gjpmt,gjpmw->tw", value_table, returned, preferred_element_type=jnp.float32
    )
    return (
        token_grads.astype(jnp.bfloat16)[None],
        query_grads[None],
        key_sum.astype(jnp.bfloat16)[None],
        value_grads.astype(jnp.bfloat16),
        output_grads.astype(jnp.bfloat16),
    )


def exchanged(
    tokens,
    cotangent,
    queries,
    key_vectors,
    value_routes,
    output_routes,
    value_experts,
    output_experts,
):
    dp_count = lax.axis_size("dp")
    dp_index = lax.axis_index("dp")
    expert_count = lax.axis_size("expert")
    expert_index = lax.axis_index("expert")
    sources = lax.axis_size("head") * expert_count
    tok_rows = tokens.shape[1]
    width = tokens.shape[2] // dp_count
    groups = queries.shape[2]
    head_dim = queries.shape[3]
    seq_len = value_routes.shape[2]
    pairs_dev = value_experts.shape[0]
    own_heads = groups // expert_count
    score_scale = head_dim ** (-0.5)
    rows = jnp.stack([tokens[0], cotangent[0]])
    rows = lax.all_to_all(rows, "dp", split_axis=2, concat_axis=1, tiled=True)
    rows = lax.all_gather(
        rows.reshape(2, dp_count, tok_rows, width), ("head", "expert"), axis=2, tiled=True
    )
    token_rows = rows[0].reshape(dp_count * seq_len, width)
    cotangent_rows = rows[1].reshape(dp_count * seq_len, width)
    routes = jnp.stack([value_routes[0, :, :, 0], output_routes[0, :, :, 0]])
    routes = lax.dynamic_slice_in_dim(routes, expert_index * own_heads, own_heads, 1)
    routes = lax.all_gather(routes, "dp", axis=1)
    picks = jnp.moveaxis(routes, 3, 2)[..., None] == jnp.arange(E, dtype=jnp.int32)
    picks = picks.reshape(2, dp_count * seq_len, own_heads, E, 1)
    pair = jnp.stack([queries[0], key_vectors[0]])
    pair = lax.all_to_all(pair, "expert", split_axis=2, concat_axis=1, tiled=True)
    query_all, key_all = (pair[0], pair[1])
    value_weight = lax.dynamic_slice_in_dim(value_experts, dp_index * width, width, 1)
    output_weight = lax.dynamic_slice_in_dim(output_experts, dp_index * width, width, 1)

    def project(source_rows, weight, pick):
        every = jnp.einsum("td,pdk->tpk", source_rows, weight, preferred_element_type=jnp.float32)
        every = every.reshape(dp_count * seq_len, own_heads, E, head_dim)
        return jnp.sum(jnp.where(pick, every, 0.0), axis=2).astype(jnp.bfloat16)

    part = jnp.stack(
        [
            project(token_rows, value_weight, picks[0]).reshape(
                dp_count, seq_len, own_heads, head_dim
            ),
            project(cotangent_rows, output_weight, picks[1]).reshape(
                dp_count, seq_len, own_heads, head_dim
            ),
        ],
        axis=1,
    )
    part = lax.all_to_all(part, "dp", split_axis=0, concat_axis=0, tiled=True)
    whole = jnp.sum(part.astype(jnp.float32), axis=0).astype(jnp.bfloat16)
    values, upstream = (whole[0], whole[1])
    scores = (
        jnp.einsum("ihc,jhc->hij", query_all, key_all, preferred_element_type=jnp.float32)
        * score_scale
    )
    position = jnp.arange(seq_len, dtype=jnp.int32)
    causal = position[None, :] <= position[:, None]
    row_top = jnp.max(jnp.where(causal, scores, -jnp.inf), axis=-1, keepdims=True)
    weights = jnp.where(causal, jnp.exp(scores - row_top), 0.0)
    probs = weights / jnp.sum(weights, axis=-1, keepdims=True)
    prob_half = probs.astype(jnp.bfloat16)
    outputs = jnp.einsum(
        "hij,jhc->ihc", prob_half, values, preferred_element_type=jnp.float32
    ).astype(jnp.bfloat16)
    row_delta = jnp.sum(outputs.astype(jnp.float32) * upstream.astype(jnp.float32), axis=-1)
    prob_grads = jnp.einsum("ihc,jhc->hij", upstream, values, preferred_element_type=jnp.float32)
    value_half = jnp.einsum(
        "hij,ihc->jhc", prob_half, upstream, preferred_element_type=jnp.float32
    ).astype(jnp.bfloat16)
    score_grads = (probs * (prob_grads - row_delta.T[:, :, None])).astype(jnp.bfloat16)
    query_grads = (
        jnp.einsum("hij,jhc->ihc", score_grads, key_all, preferred_element_type=jnp.float32)
        * score_scale
    ).astype(jnp.bfloat16)
    key_grads = (
        jnp.einsum("hij,ihc->jhc", score_grads, query_all, preferred_element_type=jnp.float32)
        * score_scale
    ).astype(jnp.bfloat16)
    factors = lax.all_gather(jnp.stack([value_half, outputs]), "dp", axis=1)
    factors = factors.reshape(2, dp_count * seq_len, own_heads, 1, head_dim)
    factors = jnp.where(picks, factors, jnp.zeros((), jnp.bfloat16)).reshape(
        2, dp_count * seq_len, pairs_dev, head_dim
    )
    token_part = jnp.einsum(
        "tpk,pdk->td", factors[0], value_weight, preferred_element_type=jnp.float32
    ).astype(jnp.bfloat16)
    token_part = lax.all_to_all(
        token_part.reshape(dp_count * sources, tok_rows, width),
        ("dp", "head", "expert"),
        split_axis=0,
        concat_axis=0,
        tiled=True,
    )
    token_grads = jnp.sum(
        token_part.reshape(dp_count, sources, tok_rows, width).astype(jnp.float32), axis=1
    ).astype(jnp.bfloat16)
    token_grads = jnp.moveaxis(token_grads, 0, 1).reshape(tok_rows, dp_count * width)
    value_grads = jnp.einsum(
        "td,tpk->pdk", token_rows, factors[0], preferred_element_type=jnp.float32
    ).astype(jnp.bfloat16)
    output_grads = jnp.einsum(
        "td,tpk->pdk", cotangent_rows, factors[1], preferred_element_type=jnp.float32
    ).astype(jnp.bfloat16)
    back = lax.all_to_all(
        jnp.stack([query_grads, key_grads]), "expert", split_axis=1, concat_axis=2, tiled=True
    )
    return (token_grads[None], back[0][None], back[1][None], value_grads, output_grads)


def chosen(*args):
    groups, pairs_dev = (args[2].shape[2], args[6].shape[0])
    expert_count = lax.axis_size("expert")
    whole_heads = groups % expert_count == 0 and pairs_dev == groups // expert_count * E
    if whole_heads and args[0].shape[2] % (lax.axis_size("dp") * 128) == 0:
        return exchanged(*args)
    return local(*args)


def solution(mesh):
    return jax.shard_map(
        chosen,
        mesh=mesh,
        in_specs=(
            P("dp", ("head", "expert"), None),
            P("dp", ("head", "expert"), None),
            P("dp", "expert", "head", None),
            P("dp", "expert", "head", None),
            P("dp", "head", None, None),
            P("dp", "head", None, None),
            P(("head", "expert"), None, None),
            P(("head", "expert"), None, None),
        ),
        out_specs=(
            P("dp", ("head", "expert"), None),
            P("dp", "expert", "head", None),
            P("dp", "expert", "head", None),
            P(("head", "expert"), "dp", None),
            P(("head", "expert"), "dp", None),
        ),
        check_vma=False,
    )
```

profile of v0, /device:TPU:0, one launch (start us, length us, event | category | flops | bytes accessed | tf_op | source)
XLA Modules:
  0.0 138.1 jit_solution(9172476691813793022)
XLA Ops:
  8.1 2.8 %copy.61 = bf16[2,8,4096]{1,0,2:T(2,128)(2,1)S(1)} copy(bf16[2,8,4096]{2,1,0:T(8,128)(2,1)S(1)} %pad_maximum_fusion.2) | data formatting | bytes 262144 | tf_op jit(solution)/shard_map/stack | solution.py:222
  10.9 2.2 %reshape.83 = bf16[4,2,8192]{2,1,0:T(2,128)(2,1)S(1)} reshape(bf16[4096,2,8]{2,1,0:T(2,128)(2,1)S(1)} %bitcast.116) | data formatting | bytes 262144
  13.2 8.6 %all_to_all.55 = bf16[4,2,8192]{2,1,0:T(2,128)(2,1)S(1)} all-to-all(bf16[4,2,8192]{2,1,0:T(2,128)(2,1)S(1)} %reshape.83), channel_id=1, replica_groups=mesh['dp'=4,'head'=4,'expert'=2] {'dp'}, dimensions={0} | all-to-all | bytes 262144 | tf_op jit(solution)/shard_map/all_to_all | solution.py:223
  21.8 2.4 %reshape.84 = bf16[4096,2,8]{2,1,0:T(2,128)(2,1)S(1)} reshape(bf16[4,2,8192]{2,1,0:T(2,128)(2,1)S(1)} %all_to_all.55) | data formatting | bytes 262144
  24.2 3.2 %copy.62 = bf16[2,8,4,1024]{3,1,2,0:T(8,128)(2,1)} copy(bf16[2,8,4,1024]{1,0,3,2:T(2,128)(2,1)S(1)} %bitcast.117) | data formatting | bytes 262144 | tf_op jit(solution)/shard_map/all_to_all | solution.py:223
  28.2 3.4 %all-to-all-start.2 = ((bf16[2,32,8,128]{3,1,0,2:T(8,128)(2,1)}), bf16[2,32,8,128]{3,1,0,2:T(8,128)(2,1)S(1)}, u32[]{:S(2)}, u32[]{:S(2)}) async-start(bf16[2,32,8,128]{3,1,0,2:T(8,128)(2,1)} %pad_maximum_fusion.1), calls=%async_computation.2 | async-start | bytes 262144 | tf_op jit(solution)/shard_map/all_to_all | solution.py:235
  31.6 5.2 %all-gather = s32[2,16,64]{2,0,1:T(2,128)S(1)} all-gather(s32[2,4,64]{2,0,1:T(2,128)S(1)} %fusion.17), channel_id=2, replica_groups=mesh['dp'=4,'head'=4,'expert'=2] {'dp'}, dimensions={1}, use_global_device_ids=true | all-gather | bytes 10240 | tf_op jit(solution)/shard_map/all_gather | solution.py:231
  37.2 7.8 %constant_dynamic-slice_fusion = (bf16[16,1024,128]{2,1,0:T(8,128)(2,1)}, bf16[16,1024,128]{2,1,0:T(8,128)(2,1)}) fusion(bf16[16,4096,128]{2,1,0:T(8,128)(2,1)} %param.15, s32[]{:T(128)S(6)} %select_n.26, bf16[16,4096,128]{2,1,0:T(8,128)(2,1)} %param.14), kind=kLoop, calls=%fused_computation.48 | loop fusion | bytes 16777220 | tf_op jit(solution)/shard_map/dynamic_slice | solution.py:238
  45.0 23.2 %all-gather.4.cloned.1.call-done = bf16[2,4,64,1024]{3,2,1,0:T(8,128)(2,1)} async-done(((bf16[2,4,8,1024]{3,2,1,0:T(8,128)(2,1)}), bf16[2,4,64,1024]{3,2,1,0:T(8,128)(2,1)}) %all-gather.4.cloned.1.call-update) | async-done | bytes 1048592 | tf_op jit(solution)/shard_map/all_gather | solution.py:224
  68.2 1.3 fusion.30
  69.5 3.3 %select_reduce_fusion = bf16[256,4,128]{2,0,1:T(8,128)(2,1)S(1)} fusion(bf16[256,1024,1,1]{1,0,3,2:T(8,128)(2,1)S(1)} %bitcast.125, bf16[4,4,128,1024]{2,3,1,0:T(8,128)(2,1)} %bitcast.119, pred[256,4,4]{0,2,1:T(4,128)(4,1)S(1)} %broadcast_in_dim.69), kind=kOutput, calls=%fused_computation.3 | convolution fusion | flops 1074659328 | bytes 4984832 | tf_op jit(solution)/shard_map/td,pdk->tpk/dot_general | solution.py:241
  73.2 1.5 %select_reduce_fusion.1 = bf16[256,4,128]{2,0,1:T(8,128)(2,1)S(1)} fusion(bf16[256,1024,1,1]{1,0,3,2:T(8,128)(2,1)S(1)} %bitcast.123, bf16[4,4,128,1024]{2,3,1,0:T(8,128)(2,1)S(1)} %bitcast.118, pred[256,4,4]{0,2,1:T(4,128)(4,1)S(1)} %broadcast_in_dim.66), kind=kOutput, calls=%fused_computation.4 | convolution fusion | flops 1074659328 | bytes 4984832 | tf_op jit(solution)/shard_map/td,pdk->tpk/dot_general | solution.py:241
  75.0 1.1 pad_maximum_fusion
  76.1 3.5 %all-to-all-start.1 = ((bf16[4,2,64,4,128]{4,3,2,1,0:T(4,128)(2,1)}), bf16[4,2,64,4,128]{4,3,2,1,0:T(4,128)(2,1)S(1)}, u32[]{:S(2)}, u32[]{:S(2)}) async-start(bf16[4,2,64,4,128]{4,3,2,1,0:T(4,128)(2,1)} %pad_maximum_fusion), calls=%async_computation.1 | async-start | bytes 1048576 | tf_op jit(solution)/shard_map/all_to_all | solution.py:256
  79.8 8.5 %all-to-all-done.1 = bf16[4,2,64,4,128]{4,3,2,1,0:T(4,128)(2,1)S(1)} async-done(((bf16[4,2,64,4,128]{4,3,2,1,0:T(4,128)(2,1)}), bf16[4,2,64,4,128]{4,3,2,1,0:T(4,128)(2,1)S(1)}, u32[]{:S(2)}, u32[]{:S(2)}) %all-to-all-start.1) | async-done | bytes 524320 | tf_op jit(solution)/shard_map/all_to_all | solution.py:256
  90.6 3.4 %all-to-all-start.4 = ((bf16[2,64,4,128]{3,2,0,1:T(4,128)(2,1)}), bf16[2,64,4,128]{3,2,0,1:T(4,128)(2,1)S(1)}, u32[]{:S(2)}, u32[]{:S(2)}) async-start(bf16[2,64,4,128]{3,2,0,1:T(4,128)(2,1)} %copy.75), calls=%async_computation.4 | async-start | bytes 262144 | tf_op jit(solution)/shard_map/all_to_all | solution.py:311
  94.0 6.6 %all-gather.1 = bf16[2,256,4,128]{3,1,2,0:T(8,128)(2,1)S(1)} all-gather(bf16[2,64,4,128]{3,1,2,0:T(8,128)(2,1)S(1)} %pad_maximum_fusion.3), channel_id=3, replica_groups=mesh['dp'=4,'head'=4,'expert'=2] {'dp'}, dimensions={1}, use_global_device_ids=true | all-gather | bytes 655360 | tf_op jit(solution)/shard_map/all_gather | solution.py:286
  100.6 1.4 %broadcast_select_fusion = bf16[2,256,4,4,128]{4,1,3,2,0:T(8,128)(2,1)S(1)} fusion(pred[2,256,4,4]{1,3,2,0:T(4,128)(4,1)S(1)} %iota_compare_fusion.2, bf16[2,256,4,128]{3,1,2,0:T(8,128)(2,1)S(1)} %all-gather.1), kind=kLoop, calls=%fused_computation.5 | loop fusion | flops 1048576 | bytes 2629632 | tf_op jit(solution)/shard_map/jit(_where)/select_n | solution.py:288
  102.2 2.1 %fusion.2 = bf16[32,8,1024]{2,1,0:T(8,128)(2,1)} fusion(bf16[256,16,128]{2,0,1:T(8,128)(2,1)S(1)} %bitcast.120, bf16[16,1024,128]{2,1,0:T(8,128)(2,1)S(1)} %copy-done.1), kind=kOutput, calls=%fused_computation.8 | convolution fusion | flops 1074003968 | bytes 5767168 | tf_op jit(solution)/shard_map/tpk,pdk->td/dot_general | solution.py:291
  104.3 4.6 %all-to-all-start.3 = ((bf16[32,8,1024]{2,1,0:T(8,128)(2,1)}), bf16[32,8,1024]{2,1,0:T(8,128)(2,1)S(1)}, u32[]{:S(2)}, u32[]{:S(2)}) async-start(bf16[32,8,1024]{2,1,0:T(8,128)(2,1)} %fusion.2), calls=%async_computation.3 | async-start | bytes 1048576 | tf_op jit(solution)/shard_map/all_to_all | solution.py:294
  108.9 4.3 %convert_bitcast_fusion = bf16[16,1024,128]{1,2,0:T(8,128)(2,1)} fusion(bf16[256,16,128]{2,0,1:T(8,128)(2,1)S(1)} %bitcast.122, bf16[256,1024,1]{1,0,2:T(8,128)(2,1)} %bitcast.126), kind=kOutput, calls=%fused_computation.1 | convolution fusion | flops 1075838976 | bytes 5767168 | tf_op jit(solution)/shard_map/td,tpk->pdk/dot_general | solution.py:308
  113.3 6.4 %copy.81 = bf16[16,1024,128]{2,1,0:T(8,128)(2,1)} copy(bf16[16,1024,128]{1,2,0:T(8,128)(2,1)} %convert_bitcast_fusion) | data formatting | bytes 8388608
  119.6 3.2 %convert_bitcast_fusion.1 = bf16[16,1024,128]{1,2,0:T(8,128)(2,1)} fusion(bf16[256,16,128]{2,0,1:T(8,128)(2,1)S(1)} %bitcast.121, bf16[256,1024,1]{1,0,2:T(8,128)(2,1)S(1)} %bitcast.124), kind=kOutput, calls=%fused_computation.2 | convolution fusion | flops 1075838976 | bytes 5767168 | tf_op jit(solution)/shard_map/td,tpk->pdk/dot_general | solution.py:305
  122.9 6.4 %copy.80 = bf16[16,1024,128]{2,1,0:T(8,128)(2,1)} copy(bf16[16,1024,128]{1,2,0:T(8,128)(2,1)} %convert_bitcast_fusion.1) | data formatting | bytes 8388608
  (53 shorter events, 7.1 us)
Async XLA Ops:
  7.2 61.1 %all-gather.4.cloned.1.call-start = ((), (), s32[]{:S(2)}) async-start(), calls=%async_computation.5 | async-start | bytes 1179648 | tf_op jit(solution)/shard_map/all_gather | solution.py:224
  8.1 19.4 %copy-start.3 = (bf16[1,32,8,128]{3,2,1,0:T(8,128)(2,1)S(1)}, bf16[1,32,8,128]{3,2,1,0:T(8,128)(2,1)}, u32[]{:S(2)}) copy-start(bf16[1,32,8,128]{3,2,1,0:T(8,128)(2,1)} %param.10) | copy-start | bytes 196612
  8.1 19.4 %copy-start.4 = (bf16[1,32,8,128]{3,2,1,0:T(8,128)(2,1)S(1)}, bf16[1,32,8,128]{3,2,1,0:T(8,128)(2,1)}, u32[]{:S(2)}) copy-start(bf16[1,32,8,128]{3,2,1,0:T(8,128)(2,1)} %param.11) | copy-start | bytes 196612
  10.9 20.7 %copy-start.5 = (s32[1,8,64,1]{2,3,1,0:T(1,128)S(1)}, s32[1,8,64,1]{2,3,1,0:T(1,128)}, u32[]{:S(2)}) copy-start(s32[1,8,64,1]{2,3,1,0:T(1,128)} %param.12) | copy-start | bytes 6148
  10.9 20.7 %copy-start.6 = (s32[1,8,64,1]{2,3,1,0:T(1,128)S(1)}, s32[1,8,64,1]{2,3,1,0:T(1,128)}, u32[]{:S(2)}) copy-start(s32[1,8,64,1]{2,3,1,0:T(1,128)} %param.13) | copy-start | bytes 6148
  28.2 16.8 %all-to-all-start.2 = ((bf16[2,32,8,128]{3,1,0,2:T(8,128)(2,1)}), bf16[2,32,8,128]{3,1,0,2:T(8,128)(2,1)S(1)}, u32[]{:S(2)}, u32[]{:S(2)}) async-start(bf16[2,32,8,128]{3,1,0,2:T(8,128)(2,1)} %pad_maximum_fusion.1), calls=%async_computation.2 | async-start | bytes 262144 | tf_op jit(solution)/shard_map/all_to_all | solution.py:235
  69.5 5.2 %copy-start.2 = (bf16[1,4,64,1024]{3,2,1,0:T(8,128)(2,1)}, bf16[1,4,64,1024]{3,2,1,0:T(8,128)(2,1)S(1)}, u32[]{:S(2)}) copy-start(bf16[1,4,64,1024]{3,2,1,0:T(8,128)(2,1)S(1)} %get-tuple-element.28) | copy-start | bytes 1572868
  69.5 3.6 %copy-start = (bf16[16,1024,128]{2,1,0:T(8,128)(2,1)S(1)}, bf16[16,1024,128]{2,1,0:T(8,128)(2,1)}, u32[]{:S(2)}) copy-start(bf16[16,1024,128]{2,1,0:T(8,128)(2,1)} %get-tuple-element.42) | copy-start | bytes 12582916
  76.1 12.3 %all-to-all-start.1 = ((bf16[4,2,64,4,128]{4,3,2,1,0:T(4,128)(2,1)}), bf16[4,2,64,4,128]{4,3,2,1,0:T(4,128)(2,1)S(1)}, u32[]{:S(2)}, u32[]{:S(2)}) async-start(bf16[4,2,64,4,128]{4,3,2,1,0:T(4,128)(2,1)} %pad_maximum_fusion), calls=%async_computation.1 | async-start | bytes 1048576 | tf_op jit(solution)/shard_map/all_to_all | solution.py:256
  90.6 13.7 %all-to-all-start.4 = ((bf16[2,64,4,128]{3,2,0,1:T(4,128)(2,1)}), bf16[2,64,4,128]{3,2,0,1:T(4,128)(2,1)S(1)}, u32[]{:S(2)}, u32[]{:S(2)}) async-start(bf16[2,64,4,128]{3,2,0,1:T(4,128)(2,1)} %copy.75), calls=%async_computation.4 | async-start | bytes 262144 | tf_op jit(solution)/shard_map/all_to_all | solution.py:311
  94.0 8.2 %copy-start.1 = (bf16[16,1024,128]{2,1,0:T(8,128)(2,1)S(1)}, bf16[16,1024,128]{2,1,0:T(8,128)(2,1)}, u32[]{:S(2)}) copy-start(bf16[16,1024,128]{2,1,0:T(8,128)(2,1)} %get-tuple-element.42) | copy-start | bytes 12582916
  104.3 26.3 %all-to-all-start.3 = ((bf16[32,8,1024]{2,1,0:T(8,128)(2,1)}), bf16[32,8,1024]{2,1,0:T(8,128)(2,1)S(1)}, u32[]{:S(2)}, u32[]{:S(2)}) async-start(bf16[32,8,1024]{2,1,0:T(8,128)(2,1)} %fusion.2), calls=%async_computation.3 | async-start | bytes 1048576 | tf_op jit(solution)/shard_map/all_to_all | solution.py:294
Sparse Core Ops, SparseCore 0:
  27.6 40.5 all-gather.3
where the time goes:
time: 139 us; the launch traced here: 138 us
  local copies, waits for them, and re-layouts  35.6 us (26%)
  waiting for transfers between devices  31.7 us (23%)
  blocking collectives  20.5 us (15%)
  matrix products  15.7 us (11%)
  starting transfers between devices  14.9 us (11%)
  between operations  14.4 us (10%)
  other arithmetic  5.27 us (4%)
    all_gather x1, waiting for transfers between devices, exchanged(): lax.all_gather(rows.reshape(2, dp_count, tok_rows, width), ('head', 'expe...  23.2 us
    unnamed x20, local copies, waits for them, and re-layouts  17.5 us
    all_to_all x1, blocking collectives, exchanged(): rows = lax.all_to_all(rows, 'dp', split_axis=2, concat_axis=1, tiled=True)  8.64 us
    all_to_all x1, waiting for transfers between devices, exchanged(): part = lax.all_to_all(part, 'dp', split_axis=0, concat_axis=0, tiled=True)  8.55 us
    dynamic_slice x1, local copies, waits for them, and re-layouts, exchanged(): lax.dynamic_slice_in_dim(output_experts, dp_index * width, width, 1)  7.79 us
    all_gather x1, blocking collectives, exchanged(): factors = lax.all_gather(jnp.stack([value_half, outputs]), 'dp', axis=1)  6.63 us
    all_gather x1, blocking collectives, exchanged(): routes = lax.all_gather(routes, 'dp', axis=1)  5.21 us
    dot_general x2, matrix products, project(): jnp.einsum('td,pdk->tpk', source_rows, weight, preferred_element_type=jnp...  4.89 us
  transfers between devices with their start and end apart: 5, of which 2 were waited for; matrix products, arithmetic and copies ran while one was open for 25% of the time, Pallas kernels for 0%

commit v1 on v0

--- a/solution.py
+++ b/solution.py
@@ -1,3 +1,4 @@
+import functools
 import jax
 import jax.numpy as jnp
 from jax import lax
@@ -5,6 +6,30 @@
 
 E = 4
 CAP = 3
+
+
+def write_trees(buf, axis_id):
+    later = lax.axis_size(axis_id)
+    r_now = lax.axis_index(axis_id)
+    arr_out, passed, fresh = (later, r_now, buf.shape[2])
+    panels = [(dev_i, (dev_i + 1) % arr_out) for dev_i in range(arr_out)]
+    x_now = jnp.zeros((*buf.shape[:2], arr_out * fresh, *buf.shape[3:]), buf.dtype)
+    x_now = lax.dynamic_update_slice_in_dim(x_now, buf, passed * fresh, axis=2)
+    low = known = buf
+    mixed_arr = arr_out // 2
+    copies = [(dev_i, (dev_i - 1) % arr_out) for dev_i in range(arr_out)]
+    for c in [*range(1, mixed_arr + 1)]:
+        low = lax.ppermute(low, axis_id, panels)
+        x_now = lax.dynamic_update_slice_in_dim(x_now, low, (passed - c) % arr_out * fresh, axis=2)
+        if c < arr_out - mixed_arr:
+            known = lax.ppermute(known, axis_id, copies)
+            x_now = lax.dynamic_update_slice_in_dim(
+                x_now, known, (passed + c) % arr_out * fresh, axis=2
+            )
+    return x_now
+
+
+tasks_unite = functools.partial(write_trees, axis_id=("head", "expert"))
 
 
 def slot_rank(routes):
@@ -221,9 +246,7 @@
     score_scale = head_dim ** (-0.5)
     rows = jnp.stack([tokens[0], cotangent[0]])
     rows = lax.all_to_all(rows, "dp", split_axis=2, concat_axis=1, tiled=True)
-    rows = lax.all_gather(
-        rows.reshape(2, dp_count, tok_rows, width), ("head", "expert"), axis=2, tiled=True
-    )
+    rows = tasks_unite(rows.reshape(2, dp_count, tok_rows, width))
     token_rows = rows[0].reshape(dp_count * seq_len, width)
     cotangent_rows = rows[1].reshape(dp_count * seq_len, width)
     routes = jnp.stack([value_routes[0, :, :, 0], output_routes[0, :, :, 0]])

time: 139 us -> 133 us (0.957)
  starting transfers between devices: 14.9 us -> 33.4 us
  between operations: 14.4 us -> 0.97 us
  blocking collectives: 20.5 us -> 12.1 us
  matrix products: 15.7 us -> 13.9 us
    all_gather x1 -> x0, waiting for transfers between devices: 23.2 us -> none  [exchanged(): lax.all_gather(rows.reshape(2, dp_count, tok_rows, width), ('head', 'expe...]
    ppermute x0 -> x7, waiting for transfers between devices: none -> 17.2 us  [the longest x4 17 us: write_trees(): low = lax.ppermute(low, axis_id, panels)]
    ppermute x0 -> x7, starting transfers between devices: none -> 15.3 us  [the longest x3 10.2 us: write_trees(): known = lax.ppermute(known, axis_id, copies)]
    all_to_all x1 -> x0, blocking collectives: 8.64 us -> none  [exchanged(): rows = lax.all_to_all(rows, 'dp', split_axis=2, concat_axis=1, tiled=True)]
    all_to_all x0 -> x1, waiting for transfers between devices: none -> 4.66 us  [exchanged(): rows = lax.all_to_all(rows, 'dp', split_axis=2, concat_axis=1, tiled=True)]
    all_to_all x0 -> x1, starting transfers between devices: none -> 3.33 us  [exchanged(): rows = lax.all_to_all(rows, 'dp', split_axis=2, concat_axis=1, tiled=True)]
    unnamed x20 -> x14, local copies, waits for them, and re-layouts: 17.5 us -> 20.4 us
    all_to_all x1, local copies, waits for them, and re-layouts: 3.22 us -> 1.24 us  [exchanged(): rows = lax.all_to_all(rows, 'dp', split_axis=2, concat_axis=1, tiled=True)]
  transfers between devices with their start and end apart: 5 -> 12, of which waited for: 2 -> 7; matrix products, arithmetic and copies ran while one was open for 25% -> 31% of each run, Pallas kernels for 0% -> 0%
where the time goes in v1:
time: 133 us; the launch traced here: 132 us
  local copies, waits for them, and re-layouts  35.5 us (27%)
  starting transfers between devices  33.4 us (25%)
  waiting for transfers between devices  30.4 us (23%)
  matrix products  13.9 us (10%)
  blocking collectives  12.1 us (9%)
  other arithmetic  5.94 us (4%)
    unnamed x14, local copies, waits for them, and re-layouts  20.4 us
    ppermute x4, waiting for transfers between devices, write_trees(): low = lax.ppermute(low, axis_id, panels)  17 us
    ppermute x3, starting transfers between devices, write_trees(): known = lax.ppermute(known, axis_id, copies)  10.2 us
    all_to_all x1, waiting for transfers between devices, exchanged(): part = lax.all_to_all(part, 'dp', split_axis=0, concat_axis=0, tiled=True)  8.55 us
    dynamic_slice x1, local copies, waits for them, and re-layouts, exchanged(): lax.dynamic_slice_in_dim(output_experts, dp_index * width, width, 1)  7.77 us
    all_gather x1, blocking collectives, exchanged(): factors = lax.all_gather(jnp.stack([value_half, outputs]), 'dp', axis=1)  6.63 us
    all_gather x1, blocking collectives, exchanged(): routes = lax.all_gather(routes, 'dp', axis=1)  5.48 us
    ppermute x4, starting transfers between devices, write_trees(): low = lax.ppermute(low, axis_id, panels)  5.05 us
  transfers between devices with their start and end apart: 12, of which 7 were waited for; matrix products, arithmetic and copies ran while one was open for 31% of the time, Pallas kernels for 0%

profile of v1, /device:TPU:0, one launch (start us, length us, event | category | flops | bytes accessed | tf_op | source)
XLA Modules:
  0.0 132.2 jit_solution(13692916528958874912)
XLA Ops:
  3.0 4.3 %all-to-all-start.2 = ((bf16[2,32,8,128]{3,1,0,2:T(8,128)(2,1)}), bf16[2,32,8,128]{3,1,0,2:T(8,128)(2,1)S(1)}, u32[]{:S(2)}, u32[]{:S(2)}) async-start(bf16[2,32,8,128]{3,1,0,2:T(8,128)(2,1)} %pad_maximum_fusion.1), calls=%async_computation.2 | async-start | bytes 262144 | tf_op jit(solution)/shard_map/all_to_all | solution.py:258
  8.0 5.5 %all-gather = s32[2,16,64]{2,0,1:T(2,128)S(1)} all-gather(s32[2,4,64]{2,0,1:T(2,128)S(1)} %fusion.17), channel_id=2, replica_groups=mesh['dp'=4,'head'=4,'expert'=2] {'dp'}, dimensions={1}, use_global_device_ids=true | all-gather | bytes 10240 | tf_op jit(solution)/shard_map/all_gather | solution.py:254
  14.7 2.8 %copy.61 = bf16[2,8,4096]{1,0,2:T(2,128)(2,1)S(1)} copy(bf16[2,8,4096]{2,1,0:T(8,128)(2,1)S(1)} %pad_maximum_fusion.2) | data formatting | bytes 262144 | tf_op jit(solution)/shard_map/stack | solution.py:247
  17.5 2.8 %reshape.83 = bf16[4,2,8192]{2,1,0:T(2,128)(2,1)} reshape(bf16[4096,2,8]{2,1,0:T(2,128)(2,1)S(1)} %bitcast.117) | data formatting | bytes 262144
  20.3 7.8 %constant_dynamic-slice_fusion = (bf16[16,1024,128]{2,1,0:T(8,128)(2,1)}, bf16[16,1024,128]{2,1,0:T(8,128)(2,1)}) fusion(bf16[16,4096,128]{2,1,0:T(8,128)(2,1)} %param.15, s32[]{:T(128)S(6)} %select_n.96, bf16[16,4096,128]{2,1,0:T(8,128)(2,1)} %param.14), kind=kLoop, calls=%fused_computation.48 | loop fusion | bytes 16777220 | tf_op jit(solution)/shard_map/dynamic_slice | solution.py:261
  28.1 3.3 %all-to-all-start = ((bf16[4,2,8192]{2,1,0:T(2,128)(2,1)}), bf16[4,2,8192]{2,1,0:T(2,128)(2,1)S(1)}, u32[]{:S(2)}, u32[]{:S(2)}) async-start(bf16[4,2,8192]{2,1,0:T(2,128)(2,1)} %reshape.83), calls=%async_computation | async-start | bytes 262144 | tf_op jit(solution)/shard_map/all_to_all | solution.py:248
  31.5 4.7 %all-to-all-done = bf16[4,2,8192]{2,1,0:T(2,128)(2,1)S(1)} async-done(((bf16[4,2,8192]{2,1,0:T(2,128)(2,1)}), bf16[4,2,8192]{2,1,0:T(2,128)(2,1)S(1)}, u32[]{:S(2)}, u32[]{:S(2)}) %all-to-all-start) | async-done | bytes 131104 | tf_op jit(solution)/shard_map/all_to_all | solution.py:248
  36.1 2.4 %reshape.84 = bf16[4096,2,8]{2,1,0:T(2,128)(2,1)S(1)} reshape(bf16[4,2,8192]{2,1,0:T(2,128)(2,1)S(1)} %all-to-all-done) | data formatting | bytes 262144
  41.8 3.4 %collective-permute-start.1 = (bf16[2,4,8,1024]{3,2,1,0:T(8,128)(2,1)S(1)}, bf16[2,4,8,1024]{3,2,1,0:T(8,128)(2,1)S(1)}, u32[]{:S(2)}, u32[]{:S(2)}) collective-permute-start(bf16[2,4,8,1024]{3,2,1,0:T(8,128)(2,1)S(1)} %bitcast.133), channel_id=1, source_target_pairs={{0,7},{1,0},{2,1},{3,2},{4,3},{5,4},{6,5},{7,6},{8,15},{9,8},{10,9... | collective-permute-start | bytes 393224 | tf_op jit(solution)/shard_map/ppermute | solution.py:25
  45.3 3.0 %collective-permute-done = bf16[2,4,8,1024]{3,2,1,0:T(8,128)(2,1)S(1)} collective-permute-done((bf16[2,4,8,1024]{3,2,1,0:T(8,128)(2,1)S(1)}, bf16[2,4,8,1024]{3,2,1,0:T(8,128)(2,1)S(1)}, u32[]{:S(2)}, u32[]{:S(2)}) %collective-permute-start) | collective-permute-done | bytes 131104 | tf_op jit(solution)/shard_map/ppermute | solution.py:22
  49.5 3.5 %collective-permute-start.3 = (bf16[2,4,8,1024]{3,2,1,0:T(8,128)(2,1)S(1)}, bf16[2,4,8,1024]{3,2,1,0:T(8,128)(2,1)S(1)}, u32[]{:S(2)}, u32[]{:S(2)}) collective-permute-start(bf16[2,4,8,1024]{3,2,1,0:T(8,128)(2,1)S(1)} %collective-permute-done.1), channel_id=1, source_target_pairs={{0,7},{1,0},{2,1},{3,2},{4,3},{5,4},{6,5},{7,6},{8,15},{9,8},{10,9... | collective-permute-start | bytes 393224 | tf_op jit(solution)/shard_map/ppermute | solution.py:25
  53.1 3.0 %collective-permute-done.2 = bf16[2,4,8,1024]{3,2,1,0:T(8,128)(2,1)S(1)} collective-permute-done((bf16[2,4,8,1024]{3,2,1,0:T(8,128)(2,1)S(1)}, bf16[2,4,8,1024]{3,2,1,0:T(8,128)(2,1)S(1)}, u32[]{:S(2)}, u32[]{:S(2)}) %collective-permute-start.2) | collective-permute-done | bytes 131104 | tf_op jit(solution)/shard_map/ppermute | solution.py:22
  57.6 3.3 %collective-permute-start.5 = (bf16[2,4,8,1024]{3,2,1,0:T(8,128)(2,1)S(1)}, bf16[2,4,8,1024]{3,2,1,0:T(8,128)(2,1)S(1)}, u32[]{:S(2)}, u32[]{:S(2)}) collective-permute-start(bf16[2,4,8,1024]{3,2,1,0:T(8,128)(2,1)S(1)} %collective-permute-done.3), channel_id=1, source_target_pairs={{0,7},{1,0},{2,1},{3,2},{4,3},{5,4},{6,5},{7,6},{8,15},{9,8},{10,9... | collective-permute-start | bytes 393224 | tf_op jit(solution)/shard_map/ppermute | solution.py:25
  61.0 3.0 %collective-permute-done.4 = bf16[2,4,8,1024]{3,2,1,0:T(8,128)(2,1)S(1)} collective-permute-done((bf16[2,4,8,1024]{3,2,1,0:T(8,128)(2,1)S(1)}, bf16[2,4,8,1024]{3,2,1,0:T(8,128)(2,1)S(1)}, u32[]{:S(2)}, u32[]{:S(2)}) %collective-permute-start.4) | collective-permute-done | bytes 131104 | tf_op jit(solution)/shard_map/ppermute | solution.py:22
  64.6 8.0 %collective-permute-done.6 = bf16[2,4,8,1024]{3,2,1,0:T(8,128)(2,1)S(1)} collective-permute-done((bf16[2,4,8,1024]{3,2,1,0:T(8,128)(2,1)S(1)}, bf16[2,4,8,1024]{3,2,1,0:T(8,128)(2,1)S(1)}, u32[]{:S(2)}, u32[]{:S(2)}) %collective-permute-start.6) | collective-permute-done | bytes 131104 | tf_op jit(solution)/shard_map/ppermute | solution.py:22
  78.0 3.5 %all-to-all-start.1 = ((bf16[4,2,64,4,128]{4,3,2,1,0:T(4,128)(2,1)}), bf16[4,2,64,4,128]{4,3,2,1,0:T(4,128)(2,1)S(1)}, u32[]{:S(2)}, u32[]{:S(2)}) async-start(bf16[4,2,64,4,128]{4,3,2,1,0:T(4,128)(2,1)} %pad_maximum_fusion), calls=%async_computation.1 | async-start | bytes 1048576 | tf_op jit(solution)/shard_map/all_to_all | solution.py:279
  81.7 8.6 %all-to-all-done.1 = bf16[4,2,64,4,128]{4,3,2,1,0:T(4,128)(2,1)S(1)} async-done(((bf16[4,2,64,4,128]{4,3,2,1,0:T(4,128)(2,1)}), bf16[4,2,64,4,128]{4,3,2,1,0:T(4,128)(2,1)S(1)}, u32[]{:S(2)}, u32[]{:S(2)}) %all-to-all-start.1) | async-done | bytes 524320 | tf_op jit(solution)/shard_map/all_to_all | solution.py:279
  92.5 3.4 %all-to-all-start.4 = ((bf16[2,64,4,128]{3,2,0,1:T(4,128)(2,1)}), bf16[2,64,4,128]{3,2,0,1:T(4,128)(2,1)S(1)}, u32[]{:S(2)}, u32[]{:S(2)}) async-start(bf16[2,64,4,128]{3,2,0,1:T(4,128)(2,1)} %copy.75), calls=%async_computation.4 | async-start | bytes 262144 | tf_op jit(solution)/shard_map/all_to_all | solution.py:334
  95.9 6.6 %all-gather.1 = bf16[2,256,4,128]{3,1,2,0:T(8,128)(2,1)S(1)} all-gather(bf16[2,64,4,128]{3,1,2,0:T(8,128)(2,1)S(1)} %pad_maximum_fusion.3), channel_id=3, replica_groups=mesh['dp'=4,'head'=4,'expert'=2] {'dp'}, dimensions={1}, use_global_device_ids=true | all-gather | bytes 655360 | tf_op jit(solution)/shard_map/all_gather | solution.py:309
  106.2 3.6 %all-to-all-start.3 = ((bf16[32,8,1024]{2,1,0:T(8,128)(2,1)}), bf16[32,8,1024]{2,1,0:T(8,128)(2,1)S(1)}, u32[]{:S(2)}, u32[]{:S(2)}) async-start(bf16[32,8,1024]{2,1,0:T(8,128)(2,1)} %fusion.2), calls=%async_computation.3 | async-start | bytes 1048576 | tf_op jit(solution)/shard_map/all_to_all | solution.py:317
  109.8 4.3 %convert_bitcast_fusion = bf16[16,1024,128]{1,2,0:T(8,128)(2,1)} fusion(bf16[256,16,128]{2,0,1:T(8,128)(2,1)S(1)} %bitcast.123, bf16[256,1024,1]{1,0,2:T(8,128)(2,1)} %bitcast.127), kind=kOutput, calls=%fused_computation.1 | convolution fusion | flops 1075838976 | bytes 5767168 | tf_op jit(solution)/shard_map/td,tpk->pdk/dot_general | solution.py:331
  114.2 6.4 %copy.81 = bf16[16,1024,128]{2,1,0:T(8,128)(2,1)} copy(bf16[16,1024,128]{1,2,0:T(8,128)(2,1)} %convert_bitcast_fusion) | data formatting | bytes 8388608
  120.6 3.2 %convert_bitcast_fusion.1 = bf16[16,1024,128]{1,2,0:T(8,128)(2,1)} fusion(bf16[256,16,128]{2,0,1:T(8,128)(2,1)S(1)} %bitcast.122, bf16[256,1024,1]{1,0,2:T(8,128)(2,1)S(1)} %bitcast.125), kind=kOutput, calls=%fused_computation.2 | convolution fusion | flops 1075838976 | bytes 5767168 | tf_op jit(solution)/shard_map/td,tpk->pdk/dot_general | solution.py:328
  123.8 6.4 %copy.80 = bf16[16,1024,128]{2,1,0:T(8,128)(2,1)} copy(bf16[16,1024,128]{1,2,0:T(8,128)(2,1)} %convert_bitcast_fusion.1) | data formatting | bytes 8388608
  (68 shorter events, 24.4 us)
Async XLA Ops:
  3.0 25.1 %all-to-all-start.2 = ((bf16[2,32,8,128]{3,1,0,2:T(8,128)(2,1)}), bf16[2,32,8,128]{3,1,0,2:T(8,128)(2,1)S(1)}, u32[]{:S(2)}, u32[]{:S(2)}) async-start(bf16[2,32,8,128]{3,1,0,2:T(8,128)(2,1)} %pad_maximum_fusion.1), calls=%async_computation.2 | async-start | bytes 262144 | tf_op jit(solution)/shard_map/all_to_all | solution.py:258
  28.1 8.0 %all-to-all-start = ((bf16[4,2,8192]{2,1,0:T(2,128)(2,1)}), bf16[4,2,8192]{2,1,0:T(2,128)(2,1)S(1)}, u32[]{:S(2)}, u32[]{:S(2)}) async-start(bf16[4,2,8192]{2,1,0:T(2,128)(2,1)} %reshape.83), calls=%async_computation | async-start | bytes 262144 | tf_op jit(solution)/shard_map/all_to_all | solution.py:248
  39.8 32.9 %copy-start.2 = (bf16[16,1024,128]{2,1,0:T(8,128)(2,1)S(1)}, bf16[16,1024,128]{2,1,0:T(8,128)(2,1)}, u32[]{:S(2)}) copy-start(bf16[16,1024,128]{2,1,0:T(8,128)(2,1)} %get-tuple-element.41) | copy-start | bytes 12582916
  39.8 8.5 %collective-permute-start = (bf16[2,4,8,1024]{3,2,1,0:T(8,128)(2,1)S(1)}, bf16[2,4,8,1024]{3,2,1,0:T(8,128)(2,1)S(1)}, u32[]{:S(2)}, u32[]{:S(2)}) collective-permute-start(bf16[2,4,8,1024]{3,2,1,0:T(8,128)(2,1)S(1)} %bitcast.132), channel_id=1, source_target_pairs={{0,1},{1,2},{2,3},{3,4},{4,5},{5,6},{6,7},{7,0},{8,9},{9,10},{10,1... | collective-permute-start | bytes 393224 | tf_op jit(solution)/shard_map/ppermute | solution.py:22
  41.8 7.8 %collective-permute-start.1 = (bf16[2,4,8,1024]{3,2,1,0:T(8,128)(2,1)S(1)}, bf16[2,4,8,1024]{3,2,1,0:T(8,128)(2,1)S(1)}, u32[]{:S(2)}, u32[]{:S(2)}) collective-permute-start(bf16[2,4,8,1024]{3,2,1,0:T(8,128)(2,1)S(1)} %bitcast.133), channel_id=1, source_target_pairs={{0,7},{1,0},{2,1},{3,2},{4,3},{5,4},{6,5},{7,6},{8,15},{9,8},{10,9... | collective-permute-start | bytes 393224 | tf_op jit(solution)/shard_map/ppermute | solution.py:25
  48.3 7.8 %collective-permute-start.2 = (bf16[2,4,8,1024]{3,2,1,0:T(8,128)(2,1)S(1)}, bf16[2,4,8,1024]{3,2,1,0:T(8,128)(2,1)S(1)}, u32[]{:S(2)}, u32[]{:S(2)}) collective-permute-start(bf16[2,4,8,1024]{3,2,1,0:T(8,128)(2,1)S(1)} %collective-permute-done), channel_id=1, source_target_pairs={{0,1},{1,2},{2,3},{3,4},{4,5},{5,6},{6,7},{7,0},{8,9},{9,10},{10,1... | collective-permute-start | bytes 393224 | tf_op jit(solution)/shard_map/ppermute | solution.py:22
  49.5 8.1 %collective-permute-start.3 = (bf16[2,4,8,1024]{3,2,1,0:T(8,128)(2,1)S(1)}, bf16[2,4,8,1024]{3,2,1,0:T(8,128)(2,1)S(1)}, u32[]{:S(2)}, u32[]{:S(2)}) collective-permute-start(bf16[2,4,8,1024]{3,2,1,0:T(8,128)(2,1)S(1)} %collective-permute-done.1), channel_id=1, source_target_pairs={{0,7},{1,0},{2,1},{3,2},{4,3},{5,4},{6,5},{7,6},{8,15},{9,8},{10,9... | collective-permute-start | bytes 393224 | tf_op jit(solution)/shard_map/ppermute | solution.py:25
  56.1 7.9 %collective-permute-start.4 = (bf16[2,4,8,1024]{3,2,1,0:T(8,128)(2,1)S(1)}, bf16[2,4,8,1024]{3,2,1,0:T(8,128)(2,1)S(1)}, u32[]{:S(2)}, u32[]{:S(2)}) collective-permute-start(bf16[2,4,8,1024]{3,2,1,0:T(8,128)(2,1)S(1)} %collective-permute-done.2), channel_id=1, source_target_pairs={{0,1},{1,2},{2,3},{3,4},{4,5},{5,6},{6,7},{7,0},{8,9},{9,10},{10,1... | collective-permute-start | bytes 393224 | tf_op jit(solution)/shard_map/ppermute | solution.py:22
  57.6 6.9 %collective-permute-start.5 = (bf16[2,4,8,1024]{3,2,1,0:T(8,128)(2,1)S(1)}, bf16[2,4,8,1024]{3,2,1,0:T(8,128)(2,1)S(1)}, u32[]{:S(2)}, u32[]{:S(2)}) collective-permute-start(bf16[2,4,8,1024]{3,2,1,0:T(8,128)(2,1)S(1)} %collective-permute-done.3), channel_id=1, source_target_pairs={{0,7},{1,0},{2,1},{3,2},{4,3},{5,4},{6,5},{7,6},{8,15},{9,8},{10,9... | collective-permute-start | bytes 393224 | tf_op jit(solution)/shard_map/ppermute | solution.py:25
  64.0 8.6 %collective-permute-start.6 = (bf16[2,4,8,1024]{3,2,1,0:T(8,128)(2,1)S(1)}, bf16[2,4,8,1024]{3,2,1,0:T(8,128)(2,1)S(1)}, u32[]{:S(2)}, u32[]{:S(2)}) collective-permute-start(bf16[2,4,8,1024]{3,2,1,0:T(8,128)(2,1)S(1)} %collective-permute-done.4), channel_id=1, source_target_pairs={{0,1},{1,2},{2,3},{3,4},{4,5},{5,6},{6,7},{7,0},{8,9},{9,10},{10,1... | collective-permute-start | bytes 393224 | tf_op jit(solution)/shard_map/ppermute | solution.py:22
  72.7 3.9 %copy-start.3 = (bf16[1,4,64,1024]{3,2,1,0:T(8,128)(2,1)}, bf16[1,4,64,1024]{3,2,1,0:T(8,128)(2,1)S(1)}, u32[]{:S(2)}) copy-start(bf16[1,4,64,1024]{3,2,1,0:T(8,128)(2,1)S(1)} %get-tuple-element.28) | copy-start | bytes 1572868
  72.7 2.4 %copy-start = (bf16[16,1024,128]{2,1,0:T(8,128)(2,1)S(1)}, bf16[16,1024,128]{2,1,0:T(8,128)(2,1)}, u32[]{:S(2)}) copy-start(bf16[16,1024,128]{2,1,0:T(8,128)(2,1)} %get-tuple-element.42) | copy-start | bytes 12582916
  78.0 12.3 %all-to-all-start.1 = ((bf16[4,2,64,4,128]{4,3,2,1,0:T(4,128)(2,1)}), bf16[4,2,64,4,128]{4,3,2,1,0:T(4,128)(2,1)S(1)}, u32[]{:S(2)}, u32[]{:S(2)}) async-start(bf16[4,2,64,4,128]{4,3,2,1,0:T(4,128)(2,1)} %pad_maximum_fusion), calls=%async_computation.1 | async-start | bytes 1048576 | tf_op jit(solution)/shard_map/all_to_all | solution.py:279
  92.5 13.7 %all-to-all-start.4 = ((bf16[2,64,4,128]{3,2,0,1:T(4,128)(2,1)}), bf16[2,64,4,128]{3,2,0,1:T(4,128)(2,1)S(1)}, u32[]{:S(2)}, u32[]{:S(2)}) async-start(bf16[2,64,4,128]{3,2,0,1:T(4,128)(2,1)} %copy.75), calls=%async_computation.4 | async-start | bytes 262144 | tf_op jit(solution)/shard_map/all_to_all | solution.py:334
  95.9 8.2 %copy-start.1 = (bf16[16,1024,128]{2,1,0:T(8,128)(2,1)S(1)}, bf16[16,1024,128]{2,1,0:T(8,128)(2,1)}, u32[]{:S(2)}) copy-start(bf16[16,1024,128]{2,1,0:T(8,128)(2,1)} %get-tuple-element.42) | copy-start | bytes 12582916
  106.2 25.3 %all-to-all-start.3 = ((bf16[32,8,1024]{2,1,0:T(8,128)(2,1)}), bf16[32,8,1024]{2,1,0:T(8,128)(2,1)S(1)}, u32[]{:S(2)}, u32[]{:S(2)}) async-start(bf16[32,8,1024]{2,1,0:T(8,128)(2,1)} %fusion.2), calls=%async_computation.3 | async-start | bytes 1048576 | tf_op jit(solution)/shard_map/all_to_all | solution.py:317
